TPU v7x, 32 devices: a whole 2x2x4 slice. The times are simulated.
32 devices in a mesh: groups: 2 (over y), seq: 4 (over z), mp: 2 (over x), sub: 2 (over core).
Axes of the slice: x: 2, y: 2, z: 4, core: 2. Of those that a mesh axis runs over, the one named last changes fastest.
Arguments:
- seq_in: bfloat16 [4096, 1536], P(('groups', 'seq'), ('mp', 'sub')), parts along dimension 0, may hold values from -48 to 48
- conv_gain: float32 [3, 1536], replicated, may hold values from 0.1 to 1.9
- conv_weight: bfloat16 [3, 3, 1536, 1536], P(None, None, None, ('mp', 'sub')), may hold values from -0.09375 to 0.09375
- w_q: bfloat16 [1536, 1024], P(None, 'mp'), may hold values from -0.102062073 to 0.102062073
- w_k: bfloat16 [1536, 1024], P(None, 'mp'), may hold values from -0.102062073 to 0.102062073
- w_v: bfloat16 [1536, 1024], P(None, 'mp'), may hold values from -0.15625 to 0.15625
- w_o: bfloat16 [1024, 1536], P('mp'), may hold values from -0.1875 to 0.1875
Outputs:
- seq_out: bfloat16 [4096, 1536], P(('groups', 'seq', 'sub'), 'mp'), parts along dimension 0
There are 2 independent parts, one for each index of `groups`. A program takes and returns all parts, laid end to end along the dimension named above; an argument that names none is the same for every part. Nothing has to cross between parts.
All inputs are finite; a program needn't handle non-finite values.
Results may differ from a plain program's by a relative error of at most 0.015.
Values may be sent and summed in bfloat16 or wider, within the bound.
No kernel may reach another device: no remote copies, remote signals or barrier semaphores. Data moves between devices by JAX's collectives and lax.ppermute only.
A program may use at most 128 MiB of HBM per device.

v0:
```python
import math
import jax
import jax.numpy as jnp
from jax import lax
from jax.sharding import PartitionSpec as P

HEAD = 128
LAYERS = 3
BINS_DEV = 512


def passed_along(x, axis, by):
    devices = lax.axis_size(axis)
    pairs = [(i, i + by) for i in range(devices) if 0 <= i + by < devices]
    return lax.ppermute(x, axis, pairs)


def tower_section(stream_shard, gain_row, weight_taps, dilation):
    rows_here = stream_shard.shape[0]
    gathered = lax.all_gather(stream_shard, ("mp", "sub"), axis=1, tiled=True)
    widened = gathered.astype(jnp.float32)
    normed = (
        widened * lax.rsqrt(jnp.mean(widened * widened, axis=1, keepdims=True) + 1e-06) * gain_row
    )
    hidden = jax.nn.gelu(normed).astype(jnp.bfloat16)
    tap_terms = jnp.einsum("rc,jco->jro", hidden, weight_taps, preferred_element_type=jnp.float32)
    span_rows = min(dilation, rows_here)
    hop_count = max(dilation // rows_here, 1)
    lower_part = passed_along(
        tap_terms[0, rows_here - span_rows :].astype(jnp.bfloat16), "seq", hop_count
    ).astype(jnp.float32)
    upper_part = passed_along(
        tap_terms[2, :span_rows].astype(jnp.bfloat16), "seq", -hop_count
    ).astype(jnp.float32)
    before = jnp.concatenate([lower_part, tap_terms[0, : rows_here - span_rows]], axis=0)
    after = jnp.concatenate([tap_terms[2, span_rows:], upper_part], axis=0)
    return (stream_shard.astype(jnp.float32) + before + tap_terms[1] + after).astype(jnp.bfloat16)


def per_device(seq_in, conv_gain, conv_weight, w_q, w_k, w_v, w_o):
    rows_here = seq_in.shape[0]
    dilations = (BINS_DEV // 4, BINS_DEV, 2 * BINS_DEV)
    stream = seq_in
    for section_index in range(LAYERS):
        stream = tower_section(
            stream, conv_gain[section_index], conv_weight[section_index], dilations[section_index]
        )
    query_rows = rows_here // lax.axis_size("sub")
    mp_width = w_o.shape[1] // lax.axis_size("mp")
    widest = lax.all_gather(stream, ("mp", "sub"), axis=1, tiled=True)
    query_inputs = lax.dynamic_slice_in_dim(
        widest, lax.axis_index("sub") * query_rows, query_rows, 0
    )
    residual_part = lax.dynamic_slice_in_dim(
        query_inputs, lax.axis_index("mp") * mp_width, mp_width, 1
    )
    heads_here = w_q.shape[1] // HEAD
    queries = (
        jnp.dot(query_inputs, w_q, preferred_element_type=jnp.float32)
        .astype(jnp.bfloat16)
        .reshape(query_rows, heads_here, HEAD)
    )
    keys = (
        jnp.dot(query_inputs, w_k, preferred_element_type=jnp.float32)
        .astype(jnp.bfloat16)
        .reshape(query_rows, heads_here, HEAD)
    )
    values = (
        jnp.dot(query_inputs, w_v, preferred_element_type=jnp.float32)
        .astype(jnp.bfloat16)
        .reshape(query_rows, heads_here, HEAD)
    )
    score_scale = 1.0 / math.sqrt(HEAD)
    running_top = jnp.full((heads_here, query_rows), -1e30, jnp.float32)
    running_numer = jnp.zeros((query_rows, heads_here, HEAD), jnp.float32)
    key_rows = lax.all_gather(keys, ("seq", "sub"), axis=0, tiled=True)
    value_rows = lax.all_gather(values, ("seq", "sub"), axis=0, tiled=True)
    scores = (
        jnp.einsum("qhe,khe->hqk", queries, key_rows, preferred_element_type=jnp.float32)
        * score_scale
    )
    new_top = jnp.maximum(running_top, jnp.max(scores, axis=-1))
    expw = jnp.exp(scores - new_top[:, :, None])
    factor = jnp.exp(running_top - new_top)
    new_denom = jnp.sum(expw, axis=-1)
    contrib = jnp.einsum(
        "hqk,khe->qhe", expw.astype(jnp.bfloat16), value_rows, preferred_element_type=jnp.float32
    )
    new_numer = running_numer * factor.T[:, :, None] + contrib
    attended = (
        (new_numer / new_denom.T[:, :, None])
        .astype(jnp.bfloat16)
        .reshape(query_rows, heads_here * HEAD)
    )
    column_weight = lax.all_to_all(w_o, "mp", split_axis=1, concat_axis=0, tiled=True)
    every_head = lax.all_gather(attended, "mp", axis=1, tiled=True)
    shares = jnp.dot(every_head, column_weight, preferred_element_type=jnp.float32)
    return (residual_part.astype(jnp.float32) + shares).astype(jnp.bfloat16)


def solution(mesh):
    placed = (
        P(("groups", "seq"), ("mp", "sub")),
        P(),
        P(None, None, None, ("mp", "sub")),
        P(None, "mp"),
        P(None, "mp"),
        P(None, "mp"),
        P("mp", None),
    )
    return jax.shard_map(
        per_device,
        mesh=mesh,
        in_specs=placed,
        out_specs=P(("groups", "seq", "sub"), "mp"),
        check_vma=False,
    )
```

profile of v0, /device:TPU:8, one launch (start us, length us, event | category | flops | bytes accessed | tf_op | source)
XLA Modules:
  0.0 252.6 jit_solution(15815357984765979070)
XLA Ops:
  6.5 0.0 copy-start
  6.5 0.0 all-gather.7.cloned.1.call-start
  6.5 0.7 all-gather.7.cloned.1.call-update
  7.3 0.0 all-gather.9.cloned.1.call-start
  7.3 0.9 slice_reduce_fusion
  8.2 21.5 %all-gather.7.cloned.1.call-done = bf16[512,1536]{1,0:T(8,128)(2,1)} async-done(((bf16[512,384]{1,0:T(8,128)(2,1)}), bf16[512,1536]{1,0:T(8,128)(2,1)}) %all-gather.7.cloned.1.call-update) | async-done | bytes 1572880 | tf_op jit(solution)/shard_map/all_gather | solution.py:20
  29.8 1.8 fusion.15
  31.6 5.6 %fusion.124 = (bf16[3,512,384]{2,1,0:T(8,128)(2,1)S(1)}, f32[3,512,384]{2,1,0:T(8,128)S(1)}) fusion(bf16[3,3,1536,384]{3,2,1,0:T(8,128)(2,1)} %param.9, bf16[512,1536]{1,0:T(8,128)(2,1)} %all-gather.7.cloned.1.call-done, f32[1536]{0:T(1024)S(1)} %get-tuple-element.6, f32[512]{0:T(512)S(1)} %add_rsqrt_fusion.2), kind=kOutput, calls=%fused_computation.142 | convolution fusion | flops 1821966336 | bytes 8658944 | tf_op jit(solution)/shard_map/rc,jco->jro/dot_general | solution.py:26
  37.1 0.0 copy-start.6
  37.2 3.5 %collective-permute-start = (bf16[128,384]{1,0:T(8,128)(2,1)S(1)}, bf16[128,384]{1,0:T(8,128)(2,1)S(1)}, u32[]{:S(2)}, u32[]{:S(2)}) collective-permute-start(bf16[128,384]{1,0:T(8,128)(2,1)S(1)} %get-tuple-element.15), channel_id=1, source_target_pairs={{0,4},{4,8},{8,12},{1,5},{5,9},{9,13},{2,6},{6,10},{10,14},{3,7},{... | collective-permute-start | bytes 294920 | tf_op jit(solution)/shard_map/ppermute | solution.py:15
  40.7 2.5 collective-permute-start.1
  43.2 0.1 slice_bitcast_fusion.3
  43.3 0.9 collective-permute-done
  44.2 3.1 %collective-permute-done.1 = bf16[128,384]{1,0:T(8,128)(2,1)S(1)} collective-permute-done((bf16[128,384]{1,0:T(8,128)(2,1)S(1)}, bf16[128,384]{1,0:T(8,128)(2,1)S(1)}, u32[]{:S(2)}, u32[]{:S(2)}) %collective-permute-start.1) | collective-permute-done | bytes 98336 | tf_op jit(solution)/shard_map/ppermute | solution.py:15
  47.3 0.0 copy-done.6
  47.3 0.9 fusion.101
  48.2 0.0 all-gather.9.cloned.1.call-update
  48.3 0.0 all-gather.11.cloned.1.call-start
  48.3 18.8 %all-gather.9.cloned.1.call-done = bf16[512,1536]{1,0:T(8,128)(2,1)} async-done(((bf16[512,384]{1,0:T(8,128)(2,1)}), bf16[512,1536]{1,0:T(8,128)(2,1)}) %all-gather.9.cloned.1.call-update) | async-done | bytes 1572880 | tf_op jit(solution)/shard_map/all_gather | solution.py:20
  67.1 1.8 fusion.24
  68.9 0.0 copy-start.3
  68.9 5.6 %fusion.125 = (bf16[3,512,384]{2,1,0:T(8,128)(2,1)S(1)}, f32[3,512,384]{2,1,0:T(8,128)S(1)}) fusion(bf16[3,3,1536,384]{3,2,1,0:T(8,128)(2,1)} %param.9, bf16[512,1536]{1,0:T(8,128)(2,1)} %all-gather.9.cloned.1.call-done, f32[1536]{0:T(1024)S(1)} %get-tuple-element.7, f32[512]{0:T(512)S(1)} %add_rsqrt_fusion.1), kind=kOutput, calls=%fused_computation.143 | convolution fusion | flops 1821966336 | bytes 8658944 | tf_op jit(solution)/shard_map/rc,jco->jro/dot_general | solution.py:26
  74.6 0.1 slice_bitcast_fusion.8
  74.7 3.4 %collective-permute-start.2 = (bf16[512,384]{1,0:T(8,128)(2,1)S(1)}, bf16[512,384]{1,0:T(8,128)(2,1)S(1)}, u32[]{:S(2)}, u32[]{:S(2)}) collective-permute-start(bf16[512,384]{1,0:T(8,128)(2,1)S(1)} %get-tuple-element.12), channel_id=1, source_target_pairs={{0,4},{4,8},{8,12},{1,5},{5,9},{9,13},{2,6},{6,10},{10,14},{3,7},{... | collective-permute-start | bytes 1179656 | tf_op jit(solution)/shard_map/ppermute | solution.py:15
  78.1 2.5 collective-permute-start.3
  80.6 7.3 %collective-permute-done.2 = bf16[512,384]{1,0:T(8,128)(2,1)S(1)} collective-permute-done((bf16[512,384]{1,0:T(8,128)(2,1)S(1)}, bf16[512,384]{1,0:T(8,128)(2,1)S(1)}, u32[]{:S(2)}, u32[]{:S(2)}) %collective-permute-start.2) | collective-permute-done | bytes 393248 | tf_op jit(solution)/shard_map/ppermute | solution.py:15
  87.8 3.1 %collective-permute-done.3 = bf16[512,384]{1,0:T(8,128)(2,1)S(1)} collective-permute-done((bf16[512,384]{1,0:T(8,128)(2,1)S(1)}, bf16[512,384]{1,0:T(8,128)(2,1)S(1)}, u32[]{:S(2)}, u32[]{:S(2)}) %collective-permute-start.3) | collective-permute-done | bytes 393248 | tf_op jit(solution)/shard_map/ppermute | solution.py:15
  90.9 1.0 fusion.98
  91.9 0.0 all-gather.11.cloned.1.call-update
  91.9 0.0 all-gather.13.cloned.1.call-start
  92.0 18.8 %all-gather.11.cloned.1.call-done = bf16[512,1536]{1,0:T(8,128)(2,1)} async-done(((bf16[512,384]{1,0:T(8,128)(2,1)}), bf16[512,1536]{1,0:T(8,128)(2,1)}) %all-gather.11.cloned.1.call-update) | async-done | bytes 1572880 | tf_op jit(solution)/shard_map/all_gather | solution.py:20
  110.8 1.8 fusion.33
  112.6 0.0 copy-start.4
  112.6 5.6 %fusion.126 = (bf16[3,512,384]{2,1,0:T(8,128)(2,1)S(1)}, f32[3,512,384]{2,1,0:T(8,128)S(1)}) fusion(bf16[3,3,1536,384]{3,2,1,0:T(8,128)(2,1)} %param.9, bf16[512,1536]{1,0:T(8,128)(2,1)} %all-gather.11.cloned.1.call-done, f32[1536]{0:T(1024)S(1)} %get-tuple-element.5, f32[512]{0:T(512)S(1)} %add_rsqrt_fusion), kind=kOutput, calls=%fused_computation.144 | convolution fusion | flops 1821966336 | bytes 8658944 | tf_op jit(solution)/shard_map/rc,jco->jro/dot_general | solution.py:26
  118.3 0.1 slice_bitcast_fusion.6
  118.4 4.3 %collective-permute-start.4 = (bf16[512,384]{1,0:T(8,128)(2,1)S(1)}, bf16[512,384]{1,0:T(8,128)(2,1)S(1)}, u32[]{:S(2)}, u32[]{:S(2)}) collective-permute-start(bf16[512,384]{1,0:T(8,128)(2,1)S(1)} %get-tuple-element.10), channel_id=1, source_target_pairs={{0,8},{4,12},{1,9},{5,13},{2,10},{6,14},{3,11},{7,15},{16,24},{20,... | collective-permute-start | bytes 1179656 | tf_op jit(solution)/shard_map/ppermute | solution.py:15
  122.7 1.3 collective-permute-start.5
  124.0 15.8 %collective-permute-done.4 = bf16[512,384]{1,0:T(8,128)(2,1)S(1)} collective-permute-done((bf16[512,384]{1,0:T(8,128)(2,1)S(1)}, bf16[512,384]{1,0:T(8,128)(2,1)S(1)}, u32[]{:S(2)}, u32[]{:S(2)}) %collective-permute-start.4) | collective-permute-done | bytes 393248 | tf_op jit(solution)/shard_map/ppermute | solution.py:15
  139.8 0.0 collective-permute-done.5
  139.8 1.0 fusion.95
  140.8 0.0 all-gather.13.cloned.1.call-update
  140.8 0.0 all-gather.15.cloned.1.call-start
  140.9 0.0 copy-start.5
  140.9 22.0 %all-gather.13.cloned.1.call-done = bf16[512,1536]{1,0:T(8,128)(2,1)} async-done(((bf16[512,384]{1,0:T(8,128)(2,1)}), bf16[512,1536]{1,0:T(8,128)(2,1)}) %all-gather.13.cloned.1.call-update) | async-done | bytes 1572880 | tf_op jit(solution)/shard_map/all_gather | solution.py:50
  162.9 1.7 fusion.86
  164.6 0.8 copy.29
  165.4 0.0 all-gather.15.cloned.1.call-update
  165.4 0.2 all-gather.17.cloned.1.call-start
  165.6 2.2 convolution_convert_fusion
  167.9 0.8 copy.19
  168.7 0.0 all-gather.17.cloned.1.call-update
  168.7 1.6 copy.17
  170.3 3.7 %all-to-all-start = ((bf16[512,2,768]{0,2,1:T(8,128)(2,1)}), bf16[512,2,768]{0,2,1:T(8,128)(2,1)S(1)}, u32[]{:S(2)}, u32[]{:S(2)}) async-start(bf16[512,2,768]{0,2,1:T(8,128)(2,1)} %bitcast.118), calls=%async_computation | async-start | bytes 3145728 | tf_op jit(solution)/shard_map/all_to_all | solution.py:95
  174.0 19.9 %all-to-all-done = bf16[512,2,768]{0,2,1:T(8,128)(2,1)S(1)} async-done(((bf16[512,2,768]{0,2,1:T(8,128)(2,1)}), bf16[512,2,768]{0,2,1:T(8,128)(2,1)S(1)}, u32[]{:S(2)}, u32[]{:S(2)}) %all-to-all-start) | async-done | bytes 1572896 | tf_op jit(solution)/shard_map/all_to_all | solution.py:95
  193.9 1.6 copy.18
  195.5 2.2 fusion.85
  197.8 0.0 all-gather.15.cloned.1.call-done
  197.8 2.9 %multiply_reduce_fusion = (f32[4,256]{1,0:T(4,128)S(1)}, f32[4,256,2048]{2,1,0:T(8,128)S(1)}) fusion(bf16[2048,4,128]{2,0,1:T(8,128)(2,1)} %all-gather.15.cloned.1.call-done, bf16[32,4,8,128]{3,2,1,0:T(8,128)(2,1)S(1)} %fusion.85), kind=kOutput, calls=%fused_computation.1 | convolution fusion | flops 541064192 | bytes 10752000 | tf_op jit(solution)/shard_map/qhe,khe->hqk/dot_general | solution.py:79
  200.7 3.2 %copy-done.1 = f32[4,256,2048]{2,1,0:T(8,128)} copy-done((f32[4,256,2048]{2,1,0:T(8,128)}, f32[4,256,2048]{2,1,0:T(8,128)S(1)}, u32[]{:S(2)}) %copy-start.1) | copy-done | bytes 8388632
  204.0 1.6 fusion
  205.6 22.7 %all-gather.17.cloned.1.call-done = bf16[2048,4,128]{0,2,1:T(8,128)(2,1)} async-done(((bf16[256,4,128]{0,2,1:T(8,128)(2,1)}), bf16[2048,4,128]{0,2,1:T(8,128)(2,1)}) %all-gather.17.cloned.1.call-update) | async-done | bytes 2097168 | tf_op jit(solution)/shard_map/all_gather | solution.py:77
  228.3 5.9 %fusion.90 = bf16[256,4,128]{0,2,1:T(8,128)(2,1)S(1)} fusion(bf16[2048,4,128]{0,2,1:T(8,128)(2,1)} %all-gather.17.cloned.1.call-done, f32[4,256,2048]{2,1,0:T(8,128)} %copy-done.1, f32[4,256]{1,0:T(4,128)S(1)} %get-tuple-element.17, f32[256,4]{0,1:T(4,128)S(1)} %bitcast.123, f32[256,4]{0,1:T(4,128)S(1)} %get-tuple-element.16), kind=kOutput, calls=%fused_computation.89 | convolution fusion | flops 543555584 | bytes 10760192 | tf_op jit(solution)/shard_map/hqk,khe->qhe/dot_general | solution.py:86
  234.2 9.1 %all_gather.27 = bf16[256,1024]{0,1:T(8,128)(2,1)S(1)} all-gather(bf16[256,512]{0,1:T(8,128)(2,1)S(1)} %bitcast.122), channel_id=1, replica_groups=mesh['groups'=2,'seq'=4,'mp'=2,'sub'=2] {'mp'}, dimensions={1}, use_global_device_ids=true | all-gather | bytes 786432 | tf_op jit(solution)/shard_map/all_gather | solution.py:96
  243.4 2.4 fusion.78
  (14 shorter events, 0.1 us)
Async XLA Ops:
  6.5 156.4 %copy-start = (bf16[1536,512]{1,0:T(8,128)(2,1)S(1)}, bf16[1536,512]{1,0:T(8,128)(2,1)}, u32[]{:S(2)}) copy-start(bf16[1536,512]{1,0:T(8,128)(2,1)} %param.11) | copy-start | bytes 4718596
  6.5 23.2 %all-gather.7.cloned.1.call-start = ((), (), s32[]{:S(2)}) async-start(), calls=%async_computation.1 | async-start | bytes 1966080 | tf_op jit(solution)/shard_map/all_gather | solution.py:20
  7.3 59.9 %all-gather.9.cloned.1.call-start = ((), (), s32[]{:S(2)}) async-start(), calls=%async_computation.2 | async-start | bytes 1966080 | tf_op jit(solution)/shard_map/all_gather | solution.py:20
  37.1 10.1 %copy-start.6 = (bf16[512,384]{1,0:T(8,128)(2,1)S(1)}, bf16[512,384]{1,0:T(8,128)(2,1)}, u32[]{:S(2)}) copy-start(bf16[512,384]{1,0:T(8,128)(2,1)} %param.7) | copy-start | bytes 1179652
  37.2 7.0 %collective-permute-start = (bf16[128,384]{1,0:T(8,128)(2,1)S(1)}, bf16[128,384]{1,0:T(8,128)(2,1)S(1)}, u32[]{:S(2)}, u32[]{:S(2)}) collective-permute-start(bf16[128,384]{1,0:T(8,128)(2,1)S(1)} %get-tuple-element.15), channel_id=1, source_target_pairs={{0,4},{4,8},{8,12},{1,5},{5,9},{9,13},{2,6},{6,10},{10,14},{3,7},{... | collective-permute-start | bytes 294920 | tf_op jit(solution)/shard_map/ppermute | solution.py:15
  40.7 6.6 %collective-permute-start.1 = (bf16[128,384]{1,0:T(8,128)(2,1)S(1)}, bf16[128,384]{1,0:T(8,128)(2,1)S(1)}, u32[]{:S(2)}, u32[]{:S(2)}) collective-permute-start(bf16[128,384]{1,0:T(8,128)(2,1)S(1)} %get-tuple-element.14), channel_id=1, source_target_pairs={{4,0},{8,4},{12,8},{5,1},{9,5},{13,9},{6,2},{10,6},{14,10},{7,3},{... | collective-permute-start | bytes 294920 | tf_op jit(solution)/shard_map/ppermute | solution.py:15
  48.3 62.5 %all-gather.11.cloned.1.call-start = ((), (), s32[]{:S(2)}) async-start(), calls=%async_computation.3 | async-start | bytes 1966080 | tf_op jit(solution)/shard_map/all_gather | solution.py:20
  68.9 22.0 %copy-start.3 = (bf16[512,384]{1,0:T(8,128)(2,1)S(1)}, bf16[512,384]{1,0:T(8,128)(2,1)}, u32[]{:S(2)}) copy-start(bf16[512,384]{1,0:T(8,128)(2,1)} %fusion.101) | copy-start | bytes 1179652
  74.7 13.1 %collective-permute-start.2 = (bf16[512,384]{1,0:T(8,128)(2,1)S(1)}, bf16[512,384]{1,0:T(8,128)(2,1)S(1)}, u32[]{:S(2)}, u32[]{:S(2)}) collective-permute-start(bf16[512,384]{1,0:T(8,128)(2,1)S(1)} %get-tuple-element.12), channel_id=1, source_target_pairs={{0,4},{4,8},{8,12},{1,5},{5,9},{9,13},{2,6},{6,10},{10,14},{3,7},{... | collective-permute-start | bytes 1179656 | tf_op jit(solution)/shard_map/ppermute | solution.py:15
  78.1 12.9 %collective-permute-start.3 = (bf16[512,384]{1,0:T(8,128)(2,1)S(1)}, bf16[512,384]{1,0:T(8,128)(2,1)S(1)}, u32[]{:S(2)}, u32[]{:S(2)}) collective-permute-start(bf16[512,384]{1,0:T(8,128)(2,1)S(1)} %get-tuple-element.13), channel_id=1, source_target_pairs={{4,0},{8,4},{12,8},{5,1},{9,5},{13,9},{6,2},{10,6},{14,10},{7,3},{... | collective-permute-start | bytes 1179656 | tf_op jit(solution)/shard_map/ppermute | solution.py:15
  91.9 71.0 %all-gather.13.cloned.1.call-start = ((), (), s32[]{:S(2)}) async-start(), calls=%async_computation.4 | async-start | bytes 1966080 | tf_op jit(solution)/shard_map/all_gather | solution.py:50
  112.6 27.2 %copy-start.4 = (bf16[512,384]{1,0:T(8,128)(2,1)S(1)}, bf16[512,384]{1,0:T(8,128)(2,1)}, u32[]{:S(2)}) copy-start(bf16[512,384]{1,0:T(8,128)(2,1)} %fusion.98) | copy-start | bytes 1179652
  118.4 21.5 %collective-permute-start.4 = (bf16[512,384]{1,0:T(8,128)(2,1)S(1)}, bf16[512,384]{1,0:T(8,128)(2,1)S(1)}, u32[]{:S(2)}, u32[]{:S(2)}) collective-permute-start(bf16[512,384]{1,0:T(8,128)(2,1)S(1)} %get-tuple-element.10), channel_id=1, source_target_pairs={{0,8},{4,12},{1,9},{5,13},{2,10},{6,14},{3,11},{7,15},{16,24},{20,... | collective-permute-start | bytes 1179656 | tf_op jit(solution)/shard_map/ppermute | solution.py:15
  122.7 17.1 %collective-permute-start.5 = (bf16[512,384]{1,0:T(8,128)(2,1)S(1)}, bf16[512,384]{1,0:T(8,128)(2,1)S(1)}, u32[]{:S(2)}, u32[]{:S(2)}) collective-permute-start(bf16[512,384]{1,0:T(8,128)(2,1)S(1)} %get-tuple-element.11), channel_id=1, source_target_pairs={{8,0},{12,4},{9,1},{13,5},{10,2},{14,6},{11,3},{15,7},{24,16},{28,... | collective-permute-start | bytes 1179656 | tf_op jit(solution)/shard_map/ppermute | solution.py:15
  140.8 57.0 %all-gather.15.cloned.1.call-start = ((), (), s32[]{:S(2)}) async-start(), calls=%async_computation.5 | async-start | bytes 2359296 | tf_op jit(solution)/shard_map/all_gather | solution.py:76
  140.9 27.8 %copy-start.5 = (bf16[512,1536]{1,0:T(8,128)(2,1)S(1)}, bf16[512,1536]{1,0:T(8,128)(2,1)}, u32[]{:S(2)}) copy-start(bf16[512,1536]{1,0:T(8,128)(2,1)} %param.13) | copy-start | bytes 4718596
  165.4 62.9 %all-gather.17.cloned.1.call-start = ((), (), s32[]{:S(2)}) async-start(), calls=%async_computation.6 | async-start | bytes 2359296 | tf_op jit(solution)/shard_map/all_gather | solution.py:77
  170.3 23.6 %all-to-all-start = ((bf16[512,2,768]{0,2,1:T(8,128)(2,1)}), bf16[512,2,768]{0,2,1:T(8,128)(2,1)S(1)}, u32[]{:S(2)}, u32[]{:S(2)}) async-start(bf16[512,2,768]{0,2,1:T(8,128)(2,1)} %bitcast.118), calls=%async_computation | async-start | bytes 3145728 | tf_op jit(solution)/shard_map/all_to_all | solution.py:95
  200.7 3.2 %copy-start.1 = (f32[4,256,2048]{2,1,0:T(8,128)}, f32[4,256,2048]{2,1,0:T(8,128)S(1)}, u32[]{:S(2)}) copy-start(f32[4,256,2048]{2,1,0:T(8,128)S(1)} %get-tuple-element.25) | copy-start | bytes 25165828
  228.3 15.1 %copy-start.2 = (bf16[2,512,768]{2,1,0:T(8,128)(2,1)S(1)}, bf16[2,512,768]{2,1,0:T(8,128)(2,1)}, u32[]{:S(2)}) copy-start(bf16[2,512,768]{2,1,0:T(8,128)(2,1)} %copy.18) | copy-start | bytes 4718596
Sparse Core Ops, SparseCore 0:
  8.9 20.7 all-gather.6
  48.4 18.7 all-gather.8
  92.1 18.7 all-gather.10
  140.9 21.9 all-gather.12
  165.5 29.0 all-gather.14
  196.1 32.1 all-gather.16
where the time goes:
time: 253 us
  waiting for transfers between devices  155 us (61%)
  matrix products  34.3 us (14%)
  starting transfers between devices  21.6 us (9%)
  between operations  13.7 us (5%)
  other arithmetic  9.91 us (4%)
  local copies, waits for them, and re-layouts  9.22 us (4%)
  blocking collectives  9.14 us (4%)
    all_gather x3, waiting for transfers between devices, tower_section(): gathered = lax.all_gather(stream_shard, ('mp', 'sub'), axis=1, tiled=True)  59.2 us
    ppermute x6, waiting for transfers between devices, passed_along(): return lax.ppermute(x, axis, pairs)  30.2 us
    all_gather x1, waiting for transfers between devices, per_device(): value_rows = lax.all_gather(values, ('seq', 'sub'), axis=0, tiled=True)  22.7 us
    all_gather x1, waiting for transfers between devices, per_device(): widest = lax.all_gather(stream, ('mp', 'sub'), axis=1, tiled=True)  22 us
    all_to_all x1, waiting for transfers between devices, per_device(): lax.all_to_all(w_o, 'mp', split_axis=1, concat_axis=0, tiled=True)  19.9 us
    ppermute x6, starting transfers between devices, passed_along(): return lax.ppermute(x, axis, pairs)  17.5 us
    dot_general x3, matrix products, tower_section(): jnp.einsum('rc,jco->jro', hidden, weight_taps, preferred_element_type=jnp...  16.9 us
    all_gather x1, blocking collectives, per_device(): every_head = lax.all_gather(attended, 'mp', axis=1, tiled=True)  9.14 us
  transfers between devices with their start and end apart: 13, of which 11 were waited for; matrix products, arithmetic and copies ran while one was open for 6% of the time, Pallas kernels for 0%

commit v1 on v0

--- a/solution.py
+++ b/solution.py
@@ -17,7 +17,29 @@
 
 def tower_section(stream_shard, gain_row, weight_taps, dilation):
     rows_here = stream_shard.shape[0]
-    gathered = lax.all_gather(stream_shard, ("mp", "sub"), axis=1, tiled=True)
+    size, index, rows = (
+        lax.axis_size(("mp", "sub")),
+        lax.axis_index(("mp", "sub")),
+        stream_shard.shape[1],
+    )
+    forward = [(i_2, (i_2 + 1) % size) for i_2 in range(size)]
+    left = [(i_2, (i_2 - 1) % size) for i_2 in range(size)]
+    gathered = jnp.zeros(
+        (*stream_shard.shape[:1], size * rows, *stream_shard.shape[1 + 1 :]), stream_shard.dtype
+    )
+    gathered = lax.dynamic_update_slice_in_dim(gathered, stream_shard, index * rows, axis=1)
+    from_left = from_right = stream_shard
+    half = size // 2
+    for step in range(1, half + 1):
+        from_left = lax.ppermute(from_left, ("mp", "sub"), forward)
+        gathered = lax.dynamic_update_slice_in_dim(
+            gathered, from_left, (index - step) % size * rows, axis=1
+        )
+        if step < size - half:
+            from_right = lax.ppermute(from_right, ("mp", "sub"), left)
+            gathered = lax.dynamic_update_slice_in_dim(
+                gathered, from_right, (index + step) % size * rows, axis=1
+            )
     widened = gathered.astype(jnp.float32)
     normed = (
         widened * lax.rsqrt(jnp.mean(widened * widened, axis=1, keepdims=True) + 1e-06) * gain_row

time: 253 us -> 228 us (0.901)
  waiting for transfers between devices: 155 us -> 131 us
  starting transfers between devices: 21.6 us -> 29.7 us
  other arithmetic: 9.91 us -> 4.24 us
  matrix products: 34.3 us -> 28.9 us
    all_gather x3 -> x0, waiting for transfers between devices: 59.2 us -> none  [tower_section(): gathered = lax.all_gather(stream_shard, ('mp', 'sub'), axis=1, tiled=True)]
    ppermute x0 -> x9, waiting for transfers between devices: none -> 34.3 us  [the longest x6 34.3 us: tower_section(): from_left = lax.ppermute(from_left, ('mp', 'sub'), forward)]
    ppermute x0 -> x9, starting transfers between devices: none -> 11.5 us  [the longest x6 7.76 us: tower_section(): from_left = lax.ppermute(from_left, ('mp', 'sub'), forward)]
    dot_general x3, matrix products: 16.9 us -> 11.5 us  [tower_section(): jnp.einsum('rc,jco->jro', hidden, weight_taps, preferred_element_type=jnp...]
    reduce_sum x3, other arithmetic: 5.37 us -> 1.15 us  [tower_section(): jnp.mean(widened * widened, axis=1, keepdims=True) + 1e-06]
    ppermute x6, starting transfers between devices: 17.5 us -> 14.4 us  [passed_along(): return lax.ppermute(x, axis, pairs)]
    all_gather x1, waiting for transfers between devices: 22 us -> 24.6 us  [per_device(): widest = lax.all_gather(stream, ('mp', 'sub'), axis=1, tiled=True)]
  transfers between devices with their start and end apart: 13 -> 19, of which waited for: 11 -> 14; matrix products, arithmetic and copies ran while one was open for 6% -> 7% of each run, Pallas kernels for 0% -> 0%
where the time goes in v1:
time: 228 us
  waiting for transfers between devices  131 us (57%)
  starting transfers between devices  29.7 us (13%)
  matrix products  28.9 us (13%)
  between operations  13.6 us (6%)
  local copies, waits for them, and re-layouts  11.2 us (5%)
  blocking collectives  9.14 us (4%)
  other arithmetic  4.24 us (2%)
    ppermute x6, waiting for transfers between devices, tower_section(): from_left = lax.ppermute(from_left, ('mp', 'sub'), forward)  34.3 us
    ppermute x6, waiting for transfers between devices, passed_along(): return lax.ppermute(x, axis, pairs)  29 us
    all_gather x1, waiting for transfers between devices, per_device(): widest = lax.all_gather(stream, ('mp', 'sub'), axis=1, tiled=True)  24.6 us
    all_gather x1, waiting for transfers between devices, per_device(): value_rows = lax.all_gather(values, ('seq', 'sub'), axis=0, tiled=True)  23 us
    all_to_all x1, waiting for transfers between devices, per_device(): lax.all_to_all(w_o, 'mp', split_axis=1, concat_axis=0, tiled=True)  19.9 us
    ppermute x6, starting transfers between devices, passed_along(): return lax.ppermute(x, axis, pairs)  14.4 us
    dot_general x3, matrix products, tower_section(): jnp.einsum('rc,jco->jro', hidden, weight_taps, preferred_element_type=jnp...  11.5 us
    all_gather x1, blocking collectives, per_device(): every_head = lax.all_gather(attended, 'mp', axis=1, tiled=True)  9.14 us
  transfers between devices with their start and end apart: 19, of which 14 were waited for; matrix products, arithmetic and copies ran while one was open for 7% of the time, Pallas kernels for 0%

profile of v1, /device:TPU:8, one launch (start us, length us, event | category | flops | bytes accessed | tf_op | source)
XLA Modules:
  0.0 227.6 jit_solution(6798353197573981971)
XLA Ops:
  6.5 1.7 collective-permute-start.1
  8.3 8.0 %collective-permute-done = bf16[512,384]{1,0:T(8,128)(2,1)S(1)} collective-permute-done((bf16[512,384]{1,0:T(8,128)(2,1)}, bf16[512,384]{1,0:T(8,128)(2,1)S(1)}, u32[]{:S(2)}, u32[]{:S(2)}) %collective-permute-start) | collective-permute-done | bytes 393248 | tf_op jit(solution)/shard_map/ppermute | solution.py:34
  16.3 0.3 collective-permute-start.2
  16.6 0.9 slice_reduce_fusion
  17.6 0.1 broadcast.71.clone.1
  17.7 1.1 constant_dynamic-update-slice_fusion.11
  18.7 0.1 constant_dynamic-update-slice_fusion.10
  18.8 0.1 constant_dynamic-update-slice_fusion.9
  18.9 4.6 %collective-permute-done.2 = bf16[512,384]{1,0:T(8,128)(2,1)S(1)} collective-permute-done((bf16[512,384]{1,0:T(8,128)(2,1)S(1)}, bf16[512,384]{1,0:T(8,128)(2,1)S(1)}, u32[]{:S(2)}, u32[]{:S(2)}) %collective-permute-start.2) | collective-permute-done | bytes 393248 | tf_op jit(solution)/shard_map/ppermute | solution.py:34
  23.5 0.1 constant_dynamic-update-slice_fusion.8
  23.6 0.4 fusion.15
  24.0 5.3 %fusion.126 = (bf16[3,512,384]{2,1,0:T(8,128)(2,1)S(1)}, f32[3,512,384]{2,1,0:T(8,128)S(1)}) fusion(bf16[3,3,1536,384]{3,2,1,0:T(8,128)(2,1)} %param.9, bf16[512,1536]{1,0:T(8,128)(2,1)S(1)} %constant_dynamic-update-slice_fusion.8, f32[1536]{0:T(1024)S(1)} %get-tuple-element.6, f32[512]{0:T(512)S(1)} %add_rsqrt_fusion.2), kind=kOutput, calls=%fused_computation.154 | convolution fusion | flops 1821966336 | bytes 8658944 | tf_op jit(solution)/shard_map/rc,jco->jro/dot_general | solution.py:48
  29.3 3.6 %collective-permute-start.3 = (bf16[128,384]{1,0:T(8,128)(2,1)S(1)}, bf16[128,384]{1,0:T(8,128)(2,1)S(1)}, u32[]{:S(2)}, u32[]{:S(2)}) collective-permute-start(bf16[128,384]{1,0:T(8,128)(2,1)S(1)} %get-tuple-element.18), channel_id=1, source_target_pairs={{0,4},{4,8},{8,12},{1,5},{5,9},{9,13},{2,6},{6,10},{10,14},{3,7},{... | collective-permute-start | bytes 294920 | tf_op jit(solution)/shard_map/ppermute | solution.py:15
  32.9 2.4 %collective-permute-start.4 = (bf16[128,384]{1,0:T(8,128)(2,1)S(1)}, bf16[128,384]{1,0:T(8,128)(2,1)S(1)}, u32[]{:S(2)}, u32[]{:S(2)}) collective-permute-start(bf16[128,384]{1,0:T(8,128)(2,1)S(1)} %get-tuple-element.19), channel_id=1, source_target_pairs={{4,0},{8,4},{12,8},{5,1},{9,5},{13,9},{6,2},{10,6},{14,10},{7,3},{... | collective-permute-start | bytes 294920 | tf_op jit(solution)/shard_map/ppermute | solution.py:15
  35.3 0.1 slice_bitcast_fusion.4
  35.4 0.8 collective-permute-done.3
  36.2 3.2 %collective-permute-done.4 = bf16[128,384]{1,0:T(8,128)(2,1)S(1)} collective-permute-done((bf16[128,384]{1,0:T(8,128)(2,1)S(1)}, bf16[128,384]{1,0:T(8,128)(2,1)S(1)}, u32[]{:S(2)}, u32[]{:S(2)}) %collective-permute-start.4) | collective-permute-done | bytes 98336 | tf_op jit(solution)/shard_map/ppermute | solution.py:15
  39.5 0.1 broadcast.71.clone
  39.6 0.2 constant_dynamic-update-slice_fusion.7
  39.9 1.7 collective-permute-start.6
  41.6 6.8 %collective-permute-done.5 = bf16[512,384]{1,0:T(8,128)(2,1)S(1)} collective-permute-done((bf16[512,384]{1,0:T(8,128)(2,1)S(1)}, bf16[512,384]{1,0:T(8,128)(2,1)S(1)}, u32[]{:S(2)}, u32[]{:S(2)}) %collective-permute-start.5) | collective-permute-done | bytes 393248 | tf_op jit(solution)/shard_map/ppermute | solution.py:34
  48.4 2.9 %collective-permute-start.7 = (bf16[512,384]{1,0:T(8,128)(2,1)S(1)}, bf16[512,384]{1,0:T(8,128)(2,1)S(1)}, u32[]{:S(2)}, u32[]{:S(2)}) collective-permute-start(bf16[512,384]{1,0:T(8,128)(2,1)S(1)} %collective-permute-done.5), channel_id=1, source_target_pairs={{0,1},{1,2},{2,3},{3,0},{4,5},{5,6},{6,7},{7,4},{8,9},{9,10},{10,1... | collective-permute-start | bytes 1179656 | tf_op jit(solution)/shard_map/ppermute | solution.py:34
  51.3 0.1 constant_dynamic-update-slice_fusion.5
  51.4 4.2 %collective-permute-done.7 = bf16[512,384]{1,0:T(8,128)(2,1)S(1)} collective-permute-done((bf16[512,384]{1,0:T(8,128)(2,1)S(1)}, bf16[512,384]{1,0:T(8,128)(2,1)S(1)}, u32[]{:S(2)}, u32[]{:S(2)}) %collective-permute-start.7) | collective-permute-done | bytes 393248 | tf_op jit(solution)/shard_map/ppermute | solution.py:34
  55.6 0.1 constant_dynamic-update-slice_fusion.4
  55.7 0.4 fusion.24
  56.1 3.1 %fusion.127 = (bf16[3,512,384]{2,1,0:T(8,128)(2,1)S(1)}, f32[3,512,384]{2,1,0:T(8,128)S(1)}) fusion(bf16[3,3,1536,384]{3,2,1,0:T(8,128)(2,1)S(1)} %bitcast.128, bf16[512,1536]{1,0:T(8,128)(2,1)S(1)} %constant_dynamic-update-slice_fusion.4, f32[1536]{0:T(1024)S(1)} %get-tuple-element.7, f32[512]{0:T(512)S(1)} %add_rsqrt_fusion.1), kind=kOutput, calls=%fused_computation.155 | convolution fusion | flops 1821966336 | bytes 8660992 | tf_op jit(solution)/shard_map/rc,jco->jro/dot_general | solution.py:48
  59.2 0.1 slice_bitcast_fusion.8
  59.3 3.5 %collective-permute-start.8 = (bf16[512,384]{1,0:T(8,128)(2,1)S(1)}, bf16[512,384]{1,0:T(8,128)(2,1)S(1)}, u32[]{:S(2)}, u32[]{:S(2)}) collective-permute-start(bf16[512,384]{1,0:T(8,128)(2,1)S(1)} %get-tuple-element.16), channel_id=1, source_target_pairs={{0,4},{4,8},{8,12},{1,5},{5,9},{9,13},{2,6},{6,10},{10,14},{3,7},{... | collective-permute-start | bytes 1179656 | tf_op jit(solution)/shard_map/ppermute | solution.py:15
  62.8 2.4 %collective-permute-start.9 = (bf16[512,384]{1,0:T(8,128)(2,1)S(1)}, bf16[512,384]{1,0:T(8,128)(2,1)S(1)}, u32[]{:S(2)}, u32[]{:S(2)}) collective-permute-start(bf16[512,384]{1,0:T(8,128)(2,1)S(1)} %get-tuple-element.17), channel_id=1, source_target_pairs={{4,0},{8,4},{12,8},{5,1},{9,5},{13,9},{6,2},{10,6},{14,10},{7,3},{... | collective-permute-start | bytes 1179656 | tf_op jit(solution)/shard_map/ppermute | solution.py:15
  65.2 6.0 %collective-permute-done.8 = bf16[512,384]{1,0:T(8,128)(2,1)S(1)} collective-permute-done((bf16[512,384]{1,0:T(8,128)(2,1)S(1)}, bf16[512,384]{1,0:T(8,128)(2,1)S(1)}, u32[]{:S(2)}, u32[]{:S(2)}) %collective-permute-start.8) | collective-permute-done | bytes 393248 | tf_op jit(solution)/shard_map/ppermute | solution.py:15
  71.2 3.8 %collective-permute-done.9 = bf16[512,384]{1,0:T(8,128)(2,1)S(1)} collective-permute-done((bf16[512,384]{1,0:T(8,128)(2,1)S(1)}, bf16[512,384]{1,0:T(8,128)(2,1)S(1)}, u32[]{:S(2)}, u32[]{:S(2)}) %collective-permute-start.9) | collective-permute-done | bytes 393248 | tf_op jit(solution)/shard_map/ppermute | solution.py:15
  75.0 0.1 broadcast.71
  75.1 0.2 constant_dynamic-update-slice_fusion.3
  75.4 1.5 collective-permute-start.10
  76.9 0.2 collective-permute-start.11
  77.2 6.6 %collective-permute-done.10 = bf16[512,384]{1,0:T(8,128)(2,1)S(1)} collective-permute-done((bf16[512,384]{1,0:T(8,128)(2,1)S(1)}, bf16[512,384]{1,0:T(8,128)(2,1)S(1)}, u32[]{:S(2)}, u32[]{:S(2)}) %collective-permute-start.10) | collective-permute-done | bytes 393248 | tf_op jit(solution)/shard_map/ppermute | solution.py:34
  83.8 3.0 %collective-permute-start.12 = (bf16[512,384]{1,0:T(8,128)(2,1)S(1)}, bf16[512,384]{1,0:T(8,128)(2,1)S(1)}, u32[]{:S(2)}, u32[]{:S(2)}) collective-permute-start(bf16[512,384]{1,0:T(8,128)(2,1)S(1)} %collective-permute-done.10), channel_id=1, source_target_pairs={{0,1},{1,2},{2,3},{3,0},{4,5},{5,6},{6,7},{7,4},{8,9},{9,10},{10,1... | collective-permute-start | bytes 1179656 | tf_op jit(solution)/shard_map/ppermute | solution.py:34
  86.9 0.1 constant_dynamic-update-slice_fusion.1
  86.9 4.1 %collective-permute-done.12 = bf16[512,384]{1,0:T(8,128)(2,1)S(1)} collective-permute-done((bf16[512,384]{1,0:T(8,128)(2,1)S(1)}, bf16[512,384]{1,0:T(8,128)(2,1)S(1)}, u32[]{:S(2)}, u32[]{:S(2)}) %collective-permute-start.12) | collective-permute-done | bytes 393248 | tf_op jit(solution)/shard_map/ppermute | solution.py:34
  91.1 0.4 fusion.33
  91.5 3.1 %fusion.128 = (bf16[3,512,384]{2,1,0:T(8,128)(2,1)S(1)}, f32[3,512,384]{2,1,0:T(8,128)S(1)}) fusion(bf16[3,3,1536,384]{3,2,1,0:T(8,128)(2,1)S(1)} %bitcast.128, bf16[512,1536]{1,0:T(8,128)(2,1)S(1)} %constant_dynamic-update-slice_fusion, f32[1536]{0:T(1024)S(1)} %get-tuple-element.5, f32[512]{0:T(512)S(1)} %add_rsqrt_fusion), kind=kOutput, calls=%fused_computation.156 | convolution fusion | flops 1821966336 | bytes 8660992 | tf_op jit(solution)/shard_map/rc,jco->jro/dot_general | solution.py:48
  94.6 0.1 slice_bitcast_fusion.6
  94.7 1.3 collective-permute-start.13
  96.1 1.3 collective-permute-start.14
  97.4 15.2 %collective-permute-done.13 = bf16[512,384]{1,0:T(8,128)(2,1)S(1)} collective-permute-done((bf16[512,384]{1,0:T(8,128)(2,1)S(1)}, bf16[512,384]{1,0:T(8,128)(2,1)S(1)}, u32[]{:S(2)}, u32[]{:S(2)}) %collective-permute-start.13) | collective-permute-done | bytes 393248 | tf_op jit(solution)/shard_map/ppermute | solution.py:15
  112.5 0.9 fusion.95
  113.5 24.6 %all-gather.4.cloned.1.call-done = bf16[512,1536]{1,0:T(8,128)(2,1)} async-done(((bf16[512,384]{1,0:T(8,128)(2,1)}), bf16[512,1536]{1,0:T(8,128)(2,1)}) %all-gather.4.cloned.1.call-update) | async-done | bytes 1572880 | tf_op jit(solution)/shard_map/all_gather | solution.py:72
  138.1 1.7 fusion.86
  139.8 0.7 copy.37
  140.6 2.2 convolution_convert_fusion
  142.9 0.8 copy.26
  143.7 1.6 copy.23
  145.3 3.7 %all-to-all-start = ((bf16[512,2,768]{0,2,1:T(8,128)(2,1)}), bf16[512,2,768]{0,2,1:T(8,128)(2,1)S(1)}, u32[]{:S(2)}, u32[]{:S(2)}) async-start(bf16[512,2,768]{0,2,1:T(8,128)(2,1)} %bitcast.121), calls=%async_computation | async-start | bytes 3145728 | tf_op jit(solution)/shard_map/all_to_all | solution.py:117
  149.0 19.9 %all-to-all-done = bf16[512,2,768]{0,2,1:T(8,128)(2,1)S(1)} async-done(((bf16[512,2,768]{0,2,1:T(8,128)(2,1)}), bf16[512,2,768]{0,2,1:T(8,128)(2,1)S(1)}, u32[]{:S(2)}, u32[]{:S(2)}) %all-to-all-start) | async-done | bytes 1572896 | tf_op jit(solution)/shard_map/all_to_all | solution.py:117
  168.9 1.6 copy.24
  170.5 2.2 fusion.85
  172.8 2.9 %multiply_reduce_fusion = (f32[4,256]{1,0:T(4,128)S(1)}, f32[4,256,2048]{2,1,0:T(8,128)S(1)}) fusion(bf16[2048,4,128]{2,0,1:T(8,128)(2,1)} %all-gather.6.cloned.1.call-done, bf16[32,4,8,128]{3,2,1,0:T(8,128)(2,1)S(1)} %fusion.85), kind=kOutput, calls=%fused_computation.1 | convolution fusion | flops 541064192 | bytes 10752000 | tf_op jit(solution)/shard_map/qhe,khe->hqk/dot_general | solution.py:101
  175.7 3.2 %copy-done.1 = f32[4,256,2048]{2,1,0:T(8,128)} copy-done((f32[4,256,2048]{2,1,0:T(8,128)}, f32[4,256,2048]{2,1,0:T(8,128)S(1)}, u32[]{:S(2)}) %copy-start.1) | copy-done | bytes 8388632
  179.0 1.6 fusion
  180.6 23.0 %all-gather.8.cloned.1.call-done = bf16[2048,4,128]{0,2,1:T(8,128)(2,1)} async-done(((bf16[256,4,128]{0,2,1:T(8,128)(2,1)}), bf16[2048,4,128]{0,2,1:T(8,128)(2,1)}) %all-gather.8.cloned.1.call-update) | async-done | bytes 2097168 | tf_op jit(solution)/shard_map/all_gather | solution.py:99
  203.6 5.9 %fusion.90 = bf16[256,4,128]{0,2,1:T(8,128)(2,1)S(1)} fusion(bf16[2048,4,128]{0,2,1:T(8,128)(2,1)} %all-gather.8.cloned.1.call-done, f32[4,256,2048]{2,1,0:T(8,128)} %copy-done.1, f32[4,256]{1,0:T(4,128)S(1)} %get-tuple-element.21, f32[256,4]{0,1:T(4,128)S(1)} %bitcast.126, f32[256,4]{0,1:T(4,128)S(1)} %get-tuple-element.20), kind=kOutput, calls=%fused_computation.89 | convolution fusion | flops 543555584 | bytes 10760192 | tf_op jit(solution)/shard_map/hqk,khe->qhe/dot_general | solution.py:108
  209.6 9.1 %all_gather.15 = bf16[256,1024]{0,1:T(8,128)(2,1)S(1)} all-gather(bf16[256,512]{0,1:T(8,128)(2,1)S(1)} %bitcast.125), channel_id=1, replica_groups=mesh['groups'=2,'seq'=4,'mp'=2,'sub'=2] {'mp'}, dimensions={1}, use_global_device_ids=true | all-gather | bytes 786432 | tf_op jit(solution)/shard_map/all_gather | solution.py:118
  218.7 2.4 %fusion.78 = bf16[256,768]{1,0:T(8,128)(2,1)} fusion(bf16[256,1024]{0,1:T(8,128)(2,1)S(1)} %all_gather.15, bf16[1024,768]{1,0:T(8,128)(2,1)S(1)} %bitcast.122, bf16[512,1536]{1,0:T(8,128)(2,1)} %all-gather.4.cloned.1.call-done, s32[]{:T(128)S(6)} %select_n.65, s32[]{:T(128)S(6)} %select_n.67), kind=kOutput, calls=%fused_computation.80 | convolution fusion | flops 403243008 | bytes 2883592 | tf_op jit(solution)/shard_map/dot_general | solution.py:119
  (39 shorter events, 0.5 us)
Async XLA Ops:
  6.5 131.6 %copy-start = (bf16[1536,512]{1,0:T(8,128)(2,1)S(1)}, bf16[1536,512]{1,0:T(8,128)(2,1)}, u32[]{:S(2)}) copy-start(bf16[1536,512]{1,0:T(8,128)(2,1)} %param.11) | copy-start | bytes 4718596
  6.5 131.6 %all-gather.4.cloned.1.call-start = ((), (), s32[]{:S(2)}) async-start(), calls=%async_computation.1 | async-start | bytes 1966080 | tf_op jit(solution)/shard_map/all_gather | solution.py:72
  6.5 9.8 %collective-permute-start = (bf16[512,384]{1,0:T(8,128)(2,1)}, bf16[512,384]{1,0:T(8,128)(2,1)S(1)}, u32[]{:S(2)}, u32[]{:S(2)}) collective-permute-start(bf16[512,384]{1,0:T(8,128)(2,1)} %param.7), channel_id=1, source_target_pairs={{0,1},{1,2},{2,3},{3,0},{4,5},{5,6},{6,7},{7,4},{8,9},{9,10},{10,1... | collective-permute-start | bytes 1179656 | tf_op jit(solution)/shard_map/ppermute | solution.py:34
  6.5 12.3 %collective-permute-start.1 = (bf16[512,384]{1,0:T(8,128)(2,1)}, bf16[512,384]{1,0:T(8,128)(2,1)S(1)}, u32[]{:S(2)}, u32[]{:S(2)}) collective-permute-start(bf16[512,384]{1,0:T(8,128)(2,1)} %param.7), channel_id=1, source_target_pairs={{0,3},{1,0},{2,1},{3,2},{4,7},{5,4},{6,5},{7,6},{8,11},{9,8},{10,9... | collective-permute-start | bytes 1179656 | tf_op jit(solution)/shard_map/ppermute | solution.py:39
  16.3 7.2 %collective-permute-start.2 = (bf16[512,384]{1,0:T(8,128)(2,1)S(1)}, bf16[512,384]{1,0:T(8,128)(2,1)S(1)}, u32[]{:S(2)}, u32[]{:S(2)}) collective-permute-start(bf16[512,384]{1,0:T(8,128)(2,1)S(1)} %collective-permute-done), channel_id=1, source_target_pairs={{0,1},{1,2},{2,3},{3,0},{4,5},{5,6},{6,7},{7,4},{8,9},{9,10},{10,1... | collective-permute-start | bytes 1179656 | tf_op jit(solution)/shard_map/ppermute | solution.py:34
  24.0 32.1 %slice-start = ((s8[10616832]{0:T(1024)(128)(4,1)}), s8[4194304]{0:T(1024)(128)(4,1)S(1)}, s32[]{:S(2)}) async-start(s8[10616832]{0:T(1024)(128)(4,1)} %bitcast.127), calls=%async_computation.4 | async-start | bytes 8388608
  24.0 32.1 %slice-start.1 = ((s8[10616832]{0:T(1024)(128)(4,1)}), s8[4194304]{0:T(1024)(128)(4,1)S(1)}, s32[]{:S(2)}) async-start(s8[10616832]{0:T(1024)(128)(4,1)} %bitcast.127), calls=%async_computation.5 | async-start | bytes 8388608
  29.3 10.3 %copy-start.4 = (bf16[512,384]{1,0:T(8,128)(2,1)S(1)}, bf16[512,384]{1,0:T(8,128)(2,1)}, u32[]{:S(2)}) copy-start(bf16[512,384]{1,0:T(8,128)(2,1)} %param.7) | copy-start | bytes 1179652
  29.3 6.9 %collective-permute-start.3 = (bf16[128,384]{1,0:T(8,128)(2,1)S(1)}, bf16[128,384]{1,0:T(8,128)(2,1)S(1)}, u32[]{:S(2)}, u32[]{:S(2)}) collective-permute-start(bf16[128,384]{1,0:T(8,128)(2,1)S(1)} %get-tuple-element.18), channel_id=1, source_target_pairs={{0,4},{4,8},{8,12},{1,5},{5,9},{9,13},{2,6},{6,10},{10,14},{3,7},{... | collective-permute-start | bytes 294920 | tf_op jit(solution)/shard_map/ppermute | solution.py:15
  32.9 6.5 %collective-permute-start.4 = (bf16[128,384]{1,0:T(8,128)(2,1)S(1)}, bf16[128,384]{1,0:T(8,128)(2,1)S(1)}, u32[]{:S(2)}, u32[]{:S(2)}) collective-permute-start(bf16[128,384]{1,0:T(8,128)(2,1)S(1)} %get-tuple-element.19), channel_id=1, source_target_pairs={{4,0},{8,4},{12,8},{5,1},{9,5},{13,9},{6,2},{10,6},{14,10},{7,3},{... | collective-permute-start | bytes 294920 | tf_op jit(solution)/shard_map/ppermute | solution.py:15
  35.3 20.8 %slice-start.2 = ((s8[10616832]{0:T(1024)(128)(4,1)}), s8[2228224]{0:T(1024)(128)(4,1)S(1)}, s32[]{:S(2)}) async-start(s8[10616832]{0:T(1024)(128)(4,1)} %bitcast.127), calls=%async_computation.6 | async-start | bytes 4456448
  39.8 8.6 %collective-permute-start.5 = (bf16[512,384]{1,0:T(8,128)(2,1)S(1)}, bf16[512,384]{1,0:T(8,128)(2,1)S(1)}, u32[]{:S(2)}, u32[]{:S(2)}) collective-permute-start(bf16[512,384]{1,0:T(8,128)(2,1)S(1)} %get-tuple-element.11), channel_id=1, source_target_pairs={{0,1},{1,2},{2,3},{3,0},{4,5},{5,6},{6,7},{7,4},{8,9},{9,10},{10,1... | collective-permute-start | bytes 1179656 | tf_op jit(solution)/shard_map/ppermute | solution.py:34
  39.9 11.4 %collective-permute-start.6 = (bf16[512,384]{1,0:T(8,128)(2,1)S(1)}, bf16[512,384]{1,0:T(8,128)(2,1)S(1)}, u32[]{:S(2)}, u32[]{:S(2)}) collective-permute-start(bf16[512,384]{1,0:T(8,128)(2,1)S(1)} %get-tuple-element.11), channel_id=1, source_target_pairs={{0,3},{1,0},{2,1},{3,2},{4,7},{5,4},{6,5},{7,6},{8,11},{9,8},{10,9... | collective-permute-start | bytes 1179656 | tf_op jit(solution)/shard_map/ppermute | solution.py:39
  48.4 7.2 %collective-permute-start.7 = (bf16[512,384]{1,0:T(8,128)(2,1)S(1)}, bf16[512,384]{1,0:T(8,128)(2,1)S(1)}, u32[]{:S(2)}, u32[]{:S(2)}) collective-permute-start(bf16[512,384]{1,0:T(8,128)(2,1)S(1)} %collective-permute-done.5), channel_id=1, source_target_pairs={{0,1},{1,2},{2,3},{3,0},{4,5},{5,6},{6,7},{7,4},{8,9},{9,10},{10,1... | collective-permute-start | bytes 1179656 | tf_op jit(solution)/shard_map/ppermute | solution.py:34
  59.3 11.9 %collective-permute-start.8 = (bf16[512,384]{1,0:T(8,128)(2,1)S(1)}, bf16[512,384]{1,0:T(8,128)(2,1)S(1)}, u32[]{:S(2)}, u32[]{:S(2)}) collective-permute-start(bf16[512,384]{1,0:T(8,128)(2,1)S(1)} %get-tuple-element.16), channel_id=1, source_target_pairs={{0,4},{4,8},{8,12},{1,5},{5,9},{9,13},{2,6},{6,10},{10,14},{3,7},{... | collective-permute-start | bytes 1179656 | tf_op jit(solution)/shard_map/ppermute | solution.py:15
  62.8 12.2 %collective-permute-start.9 = (bf16[512,384]{1,0:T(8,128)(2,1)S(1)}, bf16[512,384]{1,0:T(8,128)(2,1)S(1)}, u32[]{:S(2)}, u32[]{:S(2)}) collective-permute-start(bf16[512,384]{1,0:T(8,128)(2,1)S(1)} %get-tuple-element.17), channel_id=1, source_target_pairs={{4,0},{8,4},{12,8},{5,1},{9,5},{13,9},{6,2},{10,6},{14,10},{7,3},{... | collective-permute-start | bytes 1179656 | tf_op jit(solution)/shard_map/ppermute | solution.py:15
  75.4 8.4 %collective-permute-start.10 = (bf16[512,384]{1,0:T(8,128)(2,1)S(1)}, bf16[512,384]{1,0:T(8,128)(2,1)S(1)}, u32[]{:S(2)}, u32[]{:S(2)}) collective-permute-start(bf16[512,384]{1,0:T(8,128)(2,1)S(1)} %get-tuple-element.9), channel_id=1, source_target_pairs={{0,1},{1,2},{2,3},{3,0},{4,5},{5,6},{6,7},{7,4},{8,9},{9,10},{10,1... | collective-permute-start | bytes 1179656 | tf_op jit(solution)/shard_map/ppermute | solution.py:34
  76.9 9.9 %collective-permute-start.11 = (bf16[512,384]{1,0:T(8,128)(2,1)S(1)}, bf16[512,384]{1,0:T(8,128)(2,1)S(1)}, u32[]{:S(2)}, u32[]{:S(2)}) collective-permute-start(bf16[512,384]{1,0:T(8,128)(2,1)S(1)} %get-tuple-element.9), channel_id=1, source_target_pairs={{0,3},{1,0},{2,1},{3,2},{4,7},{5,4},{6,5},{7,6},{8,11},{9,8},{10,9... | collective-permute-start | bytes 1179656 | tf_op jit(solution)/shard_map/ppermute | solution.py:39
  83.8 7.3 %collective-permute-start.12 = (bf16[512,384]{1,0:T(8,128)(2,1)S(1)}, bf16[512,384]{1,0:T(8,128)(2,1)S(1)}, u32[]{:S(2)}, u32[]{:S(2)}) collective-permute-start(bf16[512,384]{1,0:T(8,128)(2,1)S(1)} %collective-permute-done.10), channel_id=1, source_target_pairs={{0,1},{1,2},{2,3},{3,0},{4,5},{5,6},{6,7},{7,4},{8,9},{9,10},{10,1... | collective-permute-start | bytes 1179656 | tf_op jit(solution)/shard_map/ppermute | solution.py:34
  94.7 17.8 %collective-permute-start.13 = (bf16[512,384]{1,0:T(8,128)(2,1)S(1)}, bf16[512,384]{1,0:T(8,128)(2,1)S(1)}, u32[]{:S(2)}, u32[]{:S(2)}) collective-permute-start(bf16[512,384]{1,0:T(8,128)(2,1)S(1)} %get-tuple-element.14), channel_id=1, source_target_pairs={{0,8},{4,12},{1,9},{5,13},{2,10},{6,14},{3,11},{7,15},{16,24},{20,... | collective-permute-start | bytes 1179656 | tf_op jit(solution)/shard_map/ppermute | solution.py:15
  96.1 16.5 %collective-permute-start.14 = (bf16[512,384]{1,0:T(8,128)(2,1)S(1)}, bf16[512,384]{1,0:T(8,128)(2,1)S(1)}, u32[]{:S(2)}, u32[]{:S(2)}) collective-permute-start(bf16[512,384]{1,0:T(8,128)(2,1)S(1)} %get-tuple-element.15), channel_id=1, source_target_pairs={{8,0},{12,4},{9,1},{13,5},{10,2},{14,6},{11,3},{15,7},{24,16},{28,... | collective-permute-start | bytes 1179656 | tf_op jit(solution)/shard_map/ppermute | solution.py:15
  113.5 59.3 %all-gather.6.cloned.1.call-start = ((), (), s32[]{:S(2)}) async-start(), calls=%async_computation.2 | async-start | bytes 2359296 | tf_op jit(solution)/shard_map/all_gather | solution.py:98
  139.8 3.9 %copy-start.3 = (bf16[512,1536]{1,0:T(8,128)(2,1)S(1)}, bf16[512,1536]{1,0:T(8,128)(2,1)}, u32[]{:S(2)}) copy-start(bf16[512,1536]{1,0:T(8,128)(2,1)} %param.13) | copy-start | bytes 4718596
  140.6 63.0 %all-gather.8.cloned.1.call-start = ((), (), s32[]{:S(2)}) async-start(), calls=%async_computation.3 | async-start | bytes 2359296 | tf_op jit(solution)/shard_map/all_gather | solution.py:99
  145.3 23.6 %all-to-all-start = ((bf16[512,2,768]{0,2,1:T(8,128)(2,1)}), bf16[512,2,768]{0,2,1:T(8,128)(2,1)S(1)}, u32[]{:S(2)}, u32[]{:S(2)}) async-start(bf16[512,2,768]{0,2,1:T(8,128)(2,1)} %bitcast.121), calls=%async_computation | async-start | bytes 3145728 | tf_op jit(solution)/shard_map/all_to_all | solution.py:117
  175.7 3.3 %copy-start.1 = (f32[4,256,2048]{2,1,0:T(8,128)}, f32[4,256,2048]{2,1,0:T(8,128)S(1)}, u32[]{:S(2)}) copy-start(f32[4,256,2048]{2,1,0:T(8,128)S(1)} %get-tuple-element.29) | copy-start | bytes 25165828
  203.6 15.1 %copy-start.2 = (bf16[2,512,768]{2,1,0:T(8,128)(2,1)S(1)}, bf16[2,512,768]{2,1,0:T(8,128)(2,1)}, u32[]{:S(2)}) copy-start(bf16[2,512,768]{2,1,0:T(8,128)(2,1)} %copy.24) | copy-start | bytes 4718596
Sparse Core Ops, SparseCore 0:
  113.6 24.4 all-gather.3
  140.7 29.0 all-gather.5
  171.4 32.1 all-gather.7
